TPU v7x, 256 devices: a whole 4x4x8 slice. The times are simulated.
256 devices in a mesh: gz: 8 (over x, core), gx: 32 (over z, y).
Axes of the slice: x: 4, y: 4, z: 8, core: 2. Of those that a mesh axis runs over, the one named last changes fastest.
Arguments:
- volume: float32 [256, 512, 256], P('gz', 'gx')
- measured: float32 [2, 256, 2048], P(None, 'gz')
- weight_blocks: bfloat16 [64, 128, 128], replicated, may hold values from 0 to 2
- view_order: int32 [2], replicated, may hold values from 0 to 1, each once
- tile_voxel: int32 [2, 8, 16384], P(None, 'gz', 'gx'), may hold values from 0 to 1023
- tile_column: int32 [2, 8, 16384], P(None, 'gz', 'gx'), may hold values from 0 to 15
- tile_block: int32 [2, 8, 16384], P(None, 'gz', 'gx'), may hold values from 0 to 63
- entry_count: int32 [2, 8, 32], P(None, 'gz', 'gx'), may hold values from 1 to 512, as said below
Outputs:
- volume_out: float32 [256, 512, 256], P('gz', 'gx')
Inputs may be any that keep to these rules, and one draw needn't show every extreme that they name: Entries of block (a, c) of view v at or past entry_count[v, a, c] are not used; in every view some block has 512 live entries.
All inputs are finite; a program needn't handle non-finite values.
Results may differ from a plain program's by a relative error of at most 0.0027.
Values may be sent and summed in bfloat16 or wider, within the bound.
A program may use at most 64 MiB of HBM per device.

v0:
```python
import jax
import jax.numpy as jnp
from jax import lax
from jax.sharding import PartitionSpec as P

TV_STEPS = 4
smooth_floor = 0.01
step_gain = 0.25
norm_floor = 1e-06
group_rows = 128


def padded_2(cells, sides, width):
    for axis, dim in sides:
        count = lax.axis_size(axis)
        ends = count - 1
        head = lax.slice_in_dim(cells, 0, width, axis=dim)
        tail = lax.slice_in_dim(cells, cells.shape[dim] - width, cells.shape[dim], axis=dim)
        cells = jnp.concatenate(
            [
                lax.ppermute(tail, axis, [(i, (i + 1) % count) for i in range(ends)]),
                cells,
                lax.ppermute(head, axis, [((i + 1) % count, i) for i in range(ends)]),
            ],
            axis=dim,
        )
    return cells


def tv_grad(padded):
    base_cells = padded[:-1, :-1, :-1]
    diff_z = padded[1:, :-1, :-1] - base_cells
    diff_x = padded[:-1, 1:, :-1] - base_cells
    diff_y = padded[:-1, :-1, 1:] - base_cells
    inverse = lax.rsqrt(diff_z * diff_z + diff_x * diff_x + diff_y * diff_y + smooth_floor)
    flow_z = diff_z * inverse
    flow_x = diff_x * inverse
    flow_y = diff_y * inverse
    flow_all = flow_z + flow_x + flow_y
    return flow_z[:-1, 1:, 1:] + flow_x[1:, :-1, 1:] + flow_y[1:, 1:, :-1] - flow_all[1:, 1:, 1:]


def pad_depth(field):
    return jnp.pad(field, ((0, 0), (0, 0), (1, 1)))


def body(
    volume, measured, weight_blocks, view_order, tile_voxel, tile_column, tile_block, entry_count
):
    depth_z, depth_x, depth_y = volume.shape
    tiles_y = depth_y // group_rows
    tiles_u = measured.shape[2] // group_rows
    slab_tiles = depth_z * tiles_u
    plane_tiles = depth_x * tiles_y
    row_weight = jnp.sum(weight_blocks, axis=2, dtype=jnp.float32)
    col_weight = jnp.sum(weight_blocks, axis=1, dtype=jnp.float32)
    offsets = jnp.arange(group_rows, dtype=jnp.int32)
    current = volume
    for turn_index in range(view_order.shape[0]):
        view_index = view_order[turn_index]
        voxel_list = lax.dynamic_index_in_dim(tile_voxel, view_index, 0, keepdims=False)[0]
        column_list = lax.dynamic_index_in_dim(tile_column, view_index, 0, keepdims=False)[0]
        block_list = lax.dynamic_index_in_dim(tile_block, view_index, 0, keepdims=False)[0]
        live_count = lax.dynamic_index_in_dim(entry_count, view_index, 0, keepdims=False)[0, 0]
        rounds = (live_count + group_rows - 1) // group_rows
        voxel_tiles = current.astype(jnp.bfloat16).reshape(-1, group_rows)

        def gather_group(index):
            begin = index * group_rows
            voxels = lax.dynamic_slice_in_dim(voxel_list, begin, group_rows)
            columns = lax.dynamic_slice_in_dim(column_list, begin, group_rows)
            chosen = lax.dynamic_slice_in_dim(block_list, begin, group_rows)
            weight = (begin + offsets < live_count).astype(jnp.float32)[:, None]
            detector = voxels // plane_tiles * tiles_u + columns
            return (voxels, detector, chosen, weight)

        def forward(index, carry):
            projection, ray_sum = carry
            voxels, detector, chosen, weight = gather_group(index)
            product = jnp.einsum(
                "ejk,ek->ej",
                weight_blocks[chosen],
                voxel_tiles[voxels],
                preferred_element_type=jnp.float32,
            )
            return (
                projection.at[detector].add(product * weight),
                ray_sum.at[detector].add(row_weight[chosen] * weight),
            )

        empty = jnp.zeros((slab_tiles, group_rows), jnp.float32)
        projection, ray_sum = lax.fori_loop(0, rounds, forward, (empty, empty))
        target = lax.dynamic_index_in_dim(measured, view_index, 0, keepdims=False).reshape(
            slab_tiles, group_rows
        )
        projection, ray_sum = (
            lax.psum(projection.astype(jnp.bfloat16), "gx").astype(jnp.float32),
            lax.psum(ray_sum.astype(jnp.bfloat16), "gx").astype(jnp.float32),
        )
        residual = ((target - projection) / (ray_sum + 1.0)).astype(jnp.bfloat16)

        def backward(index, carry):
            change, voxel_sum = carry
            voxels, detector, chosen, weight = gather_group(index)
            product = jnp.einsum(
                "ejk,ej->ek",
                weight_blocks[chosen],
                residual[detector],
                preferred_element_type=jnp.float32,
            )
            return (
                change.at[voxels].add(product * weight),
                voxel_sum.at[voxels].add(col_weight[chosen] * weight),
            )

        blank = jnp.zeros((voxel_tiles.shape[0], group_rows), jnp.float32)
        change, voxel_sum = lax.fori_loop(0, rounds, backward, (blank, blank))
        current = current + (change / (voxel_sum + 1.0)).reshape(current.shape)
    art_volume = jnp.maximum(current, 0.0)
    difference = art_volume - volume
    change_part = jnp.sum(difference * difference)
    change_total = None
    change_total = lax.psum(change_part, ("gz", "gx"))
    smooth = art_volume
    for sweep_index in range(TV_STEPS):
        padded = padded_2(smooth, (("gz", 0), ("gx", 1)), 1)
        slope = tv_grad(pad_depth(padded))
        slope_part = jnp.sum(slope * slope)
        if sweep_index == 0:
            slope_total = lax.psum(slope_part, ("gz", "gx"))
        else:
            slope_total = lax.psum(slope_part, ("gz", "gx"))
        change_total, scale_now = (
            change_total,
            step_gain * jnp.sqrt(change_total) / jnp.sqrt(slope_total + norm_floor),
        )
        smooth = smooth - scale_now * slope
    return smooth


def solution(mesh):
    return jax.shard_map(
        body,
        mesh=mesh,
        in_specs=(
            P("gz", "gx", None),
            P(None, "gz", None),
            P(),
            P(),
            P(None, "gz", "gx"),
            P(None, "gz", "gx"),
            P(None, "gz", "gx"),
            P(None, "gz", "gx"),
        ),
        out_specs=P("gz", "gx", None),
        check_vma=False,
    )
```

profile of v0, /device:TPU:1, one launch (start us, length us, event | category | flops | bytes accessed | tf_op | source)
XLA Modules:
  0.0 943.3 jit_solution(2549535672975663778)
XLA Ops:
  6.5 1.3 fusion.70
  11.5 1.4 constant_dynamic-slice_fusion.4
  14.3 2.4 convert_reduce_fusion
  17.6 13.5 %while.60 = (s32[]{:T(128)}, f32[512,128]{1,0:T(8,128)S(1)}, f32[512,128]{1,0:T(8,128)}, s32[]{:T(128)}, s32[512]{0:T(512)S(1)}, /*index=5*/s32[512]{0:T(512)S(1...) while((s32[]{:T(128)}, f32[512,128]{1,0:T(8,128)S(1)}, ...), condition=%wide.region_4.5_spmd.clone, body=%wide.region_1.4_spmd.clone.sunk | while | flops 4265478 | bytes 13388487 | solution.py:92
  17.7 3.0 gather_fusion
  21.5 4.4 fusion.99
  26.6 1.4 scatter_custom_fusion.42
  28.1 3.1 scatter_custom_fusion.43
  31.8 1.6 convert_element_type.89
  36.0 180.4 %all-reduce.12.cloned.1.call-done = (bf16[512,128]{1,0:T(8,128)(2,1)}, bf16[512,128]{1,0:T(8,128)(2,1)}) async-done(((bf16[512,128]{1,0:T(8,128)(2,1)}, bf16[512,128]{1,0:T(8,128)(2,1)}), (bf16[512,128]{1,0:T(8,128)(2,1)}, bf16[512,128]{1,0:T(8,128)(2,1)})) %all-reduce.12.cloned.1.call-update) | async-done | bytes 262160 | tf_op jit(solution)/shard_map/psum | solution.py:98
  219.1 14.2 %while.61 = (s32[]{:T(128)}, f32[1024,128]{1,0:T(8,128)}, f32[1024,128]{1,0:T(8,128)}, s32[]{:T(128)}, s32[512]{0:T(512)S(1)}, /*index=5*/s32[512]{0:T(512)S(1)}...) while((s32[]{:T(128)}, f32[1024,128]{1,0:T(8,128)}, ...), condition=%wide.region_11.12_spmd.clone, body=%wide.region_8.11_spmd.clone.sunk | while | flops 4265478 | bytes 13912775 | solution.py:117
  219.2 3.0 gather_fusion.2
  223.0 3.4 fusion.104
  227.0 3.1 scatter_custom_fusion.46
  230.1 3.3 scatter_custom_fusion.47
  233.4 2.1 add_divide_fusion.1
  235.4 2.0 reshape.54
  237.4 2.0 fusion.65
  241.9 14.9 %while.62 = (s32[]{:T(128)}, f32[512,128]{1,0:T(8,128)}, f32[512,128]{1,0:T(8,128)}, s32[]{:T(128)}, s32[512]{0:T(512)S(1)}, /*index=5*/s32[512]{0:T(512)S(1)}, ...) while((s32[]{:T(128)}, f32[512,128]{1,0:T(8,128)}, ...), condition=%wide.region_15.16_spmd.clone, body=%wide.region_12.15_spmd.clone.sunk | while | flops 4265478 | bytes 13388487 | solution.py:92
  242.0 3.0 gather_fusion.4
  245.7 4.4 fusion.109
  250.8 2.9 scatter_custom_fusion.50
  253.7 3.1 scatter_custom_fusion.51
  256.8 1.6 convert_element_type.93
  258.4 1.6 convert_element_type.95
  260.8 227.2 %all-reduce.10.cloned.1.call-done = (bf16[512,128]{1,0:T(8,128)(2,1)}, bf16[512,128]{1,0:T(8,128)(2,1)}) async-done(((bf16[512,128]{1,0:T(8,128)(2,1)}, bf16[512,128]{1,0:T(8,128)(2,1)}), (bf16[512,128]{1,0:T(8,128)(2,1)}, bf16[512,128]{1,0:T(8,128)(2,1)})) %all-reduce.10.cloned.1.call-update) | async-done | bytes 262160 | tf_op jit(solution)/shard_map/psum | solution.py:98
  490.0 12.7 %while.63 = (s32[]{:T(128)}, f32[1024,128]{1,0:T(8,128)S(1)}, f32[1024,128]{1,0:T(8,128)}, s32[]{:T(128)}, s32[512]{0:T(512)S(1)}, /*index=5*/s32[512]{0:T(512)S...) while((s32[]{:T(128)}, f32[1024,128]{1,0:T(8,128)S(1)}, ...), condition=%wide.region_21.22_spmd.clone, body=%wide.region_18.21_spmd.clone.sunk | while | flops 4265478 | bytes 13912775 | solution.py:117
  490.1 3.0 gather_fusion.6
  493.8 3.4 fusion.114
  497.9 1.5 scatter_custom_fusion.54
  499.4 3.3 scatter_custom_fusion.55
  502.7 1.2 add_divide_fusion
  504.9 8.1 collective-permute-start
  513.0 1.9 collective-permute-start.1
  514.9 3.1 collective-permute-done.1
  518.1 2.0 collective-permute-start.2
  520.0 1.3 collective-permute-start.3
  521.3 3.4 collective-permute-done.3
  526.5 1.4 multiply_reduce_fusion.3
  527.9 113.9 %all-reduce.4 = (f32[]{:T(128)}, f32[]{:T(128)}) all-reduce(f32[]{:T(128)} %get-tuple-element.839, f32[]{:T(128)} %get-tuple-element.837), channel_id=1, replica_groups=mesh['gz'=8,'gx'=32] {'gz','gx'}, use_global_device_ids=true, to_apply=%region_23.24 | all-reduce | flops 2 | bytes 16 | tf_op jit(solution)/shard_map/psum | solution.py:123
  643.4 3.5 collective-permute-start.4
  647.0 1.9 collective-permute-start.5
  648.9 3.1 collective-permute-done.5
  652.1 1.4 collective-permute-start.6
  653.5 1.3 collective-permute-start.7
  654.8 3.6 collective-permute-done.7
  660.2 1.4 multiply_reduce_fusion.2
  661.7 77.6 %psum.69 = f32[]{:T(128)} all-reduce(f32[]{:T(128)} %get-tuple-element.833), channel_id=1, replica_groups=mesh['gz'=8,'gx'=32] {'gz','gx'}, use_global_device_ids=true, to_apply=%region_27.28 | all-reduce | flops 1 | bytes 8 | tf_op jit(solution)/shard_map/psum | solution.py:132
  740.1 3.5 collective-permute-start.8
  743.6 1.9 collective-permute-start.9
  745.5 3.1 collective-permute-done.9
  748.7 1.4 collective-permute-start.10
  750.1 1.5 collective-permute-start.11
  751.6 3.4 collective-permute-done.11
  756.8 1.4 multiply_reduce_fusion.1
  758.3 78.8 %psum.70 = f32[]{:T(128)} all-reduce(f32[]{:T(128)} %get-tuple-element.829), channel_id=1, replica_groups=mesh['gz'=8,'gx'=32] {'gz','gx'}, use_global_device_ids=true, to_apply=%region_29.30 | all-reduce | flops 1 | bytes 8 | tf_op jit(solution)/shard_map/psum | solution.py:132
  837.8 3.5 collective-permute-start.12
  841.3 1.9 collective-permute-start.13
  843.3 3.1 collective-permute-done.13
  846.5 1.4 collective-permute-start.14
  847.9 1.3 collective-permute-start.15
  849.2 3.6 collective-permute-done.15
  854.6 1.4 multiply_reduce_fusion
  856.0 78.8 %psum.71 = f32[]{:T(128)} all-reduce(f32[]{:T(128)} %get-tuple-element.825), channel_id=1, replica_groups=mesh['gz'=8,'gx'=32] {'gz','gx'}, use_global_device_ids=true, to_apply=%region_31.32 | all-reduce | flops 1 | bytes 8 | tf_op jit(solution)/shard_map/psum | solution.py:132
  (87 shorter events, 27.6 us)
Async XLA Ops:
  6.5 10.1 %copy-start.1 = (f32[32,16,256]{2,1,0:T(8,128)S(1)}, f32[32,16,256]{2,1,0:T(8,128)}, u32[]{:S(2)}) copy-start(f32[32,16,256]{2,1,0:T(8,128)} %param.16) | copy-start | bytes 1572868
  6.5 209.8 %all-reduce.12.cloned.1.call-start = ((), (), s32[]{:S(2)}) async-start(), calls=%async_computation.1 | async-start | bytes 524288 | tf_op jit(solution)/shard_map/psum | solution.py:98
  14.3 2.6 copy-start.3
  14.3 2.6 copy-start.4
  14.3 3.4 copy-start
  33.4 454.6 %all-reduce.10.cloned.1.call-start = ((), (), s32[]{:S(2)}) async-start(), calls=%async_computation | async-start | bytes 524288 | tf_op jit(solution)/shard_map/psum | solution.py:98
  502.7 1.3 copy-start.2
  504.9 10.0 %collective-permute-start = (f32[1,16,256]{2,1,0:T(8,128)S(1)}, f32[1,16,256]{2,1,0:T(8,128)S(1)}, u32[]{:S(2)}, u32[]{:S(2)}) collective-permute-start(f32[1,16,256]{2,1,0:T(8,128)S(1)} %get-tuple-element.879), channel_id=1, source_target_pairs={{0,32},{32,64},{64,96},{96,128},{128,160},{160,192},{192,224},{1,3... | collective-permute-start | bytes 49160 | tf_op jit(solution)/shard_map/ppermute | solution.py:21
  513.0 5.1 collective-permute-start.1
  518.1 3.3 collective-permute-start.2
  520.0 4.7 collective-permute-start.3
  643.4 5.5 collective-permute-start.4
  647.0 5.1 collective-permute-start.5
  652.1 2.7 collective-permute-start.6
  653.5 4.9 collective-permute-start.7
  740.1 5.4 collective-permute-start.8
  743.6 5.1 collective-permute-start.9
  748.7 2.9 collective-permute-start.10
  750.1 4.9 collective-permute-start.11
  837.8 5.4 collective-permute-start.12
  841.3 5.1 collective-permute-start.13
  846.5 2.7 collective-permute-start.14
  847.9 4.9 collective-permute-start.15
Sparse Core Ops, SparseCore 0:
  33.6 182.7 all-reduce.11
  260.1 227.8 all-reduce.9
where the time goes:
time: 946 us; the launch traced here: 943 us
  waiting for transfers between devices  434 us (46%)
  blocking collectives  349 us (37%)
  other arithmetic  55.2 us (6%)
  starting transfers between devices  37.9 us (4%)
  local copies, waits for them, and re-layouts  28.9 us (3%)
  between operations  22.3 us (2%)
  matrix products  15.6 us (2%)
    psum x2, waiting for transfers between devices, body(): lax.psum(ray_sum.astype(jnp.bfloat16), 'gx').astype(jnp.float32)  408 us
    psum x3, blocking collectives, body(): slope_total = lax.psum(slope_part, ('gz', 'gx'))  235 us
    psum x1, blocking collectives, body(): change_total = lax.psum(change_part, ('gz', 'gx'))  114 us
    ppermute x8, waiting for transfers between devices, padded_2(): lax.ppermute(head, axis, [((i + 1) % count, i) for i in range(ends)])  26.5 us
    ppermute x8, starting transfers between devices, padded_2(): lax.ppermute(tail, axis, [(i, (i + 1) % count) for i in range(ends)])  24.8 us
  transfers between devices with their start and end apart: 18, of which 10 were waited for; matrix products, arithmetic and copies ran while one was open for 0% of the time, Pallas kernels for 0%

commit v1 on v0

--- a/solution.py
+++ b/solution.py
@@ -8,6 +8,11 @@
 step_gain = 0.25
 norm_floor = 1e-06
 group_rows = 128
+
+
+def add_all(x, mesh_axis):
+    parts = lax.all_gather(x, mesh_axis)
+    return jnp.sum(parts, axis=0)
 
 
 def padded_2(cells, sides, width):
@@ -95,7 +100,7 @@
         )
         projection, ray_sum = (
             lax.psum(projection.astype(jnp.bfloat16), "gx").astype(jnp.float32),
-            lax.psum(ray_sum.astype(jnp.bfloat16), "gx").astype(jnp.float32),
+            add_all(ray_sum.astype(jnp.bfloat16), "gx").astype(jnp.float32),
         )
         residual = ((target - projection) / (ray_sum + 1.0)).astype(jnp.bfloat16)
 

time: 946 us -> 1100 us (1.16)
  waiting for transfers between devices: 434 us -> 585 us
    all_gather x0 -> x2, waiting for transfers between devices: none -> 283 us  [add_all(): parts = lax.all_gather(x, mesh_axis)]
    psum x2, waiting for transfers between devices: 408 us -> 275 us  [body(): lax.psum(projection.astype(jnp.bfloat16), 'gx').astype(jnp.float32)]
  transfers between devices with their start and end apart: 18 -> 20, of which waited for: 10 -> 12; matrix products, arithmetic and copies ran while one was open for 0% -> 1% of each run, Pallas kernels for 0% -> 0%
where the time goes in v1:
time: 1100 us
  waiting for transfers between devices  585 us (53%)
  blocking collectives  348 us (32%)
  other arithmetic  60.5 us (6%)
  starting transfers between devices  38.6 us (4%)
  local copies, waits for them, and re-layouts  28.9 us (3%)
  between operations  22.1 us (2%)
  matrix products  15.6 us (1%)
    all_gather x2, waiting for transfers between devices, add_all(): parts = lax.all_gather(x, mesh_axis)  283 us
    psum x2, waiting for transfers between devices, body(): lax.psum(projection.astype(jnp.bfloat16), 'gx').astype(jnp.float32)  275 us
    psum x3, blocking collectives, body(): slope_total = lax.psum(slope_part, ('gz', 'gx'))  235 us
    psum x1, blocking collectives, body(): change_total = lax.psum(change_part, ('gz', 'gx'))  112 us
    ppermute x8, waiting for transfers between devices, padded_2(): lax.ppermute(head, axis, [((i + 1) % count, i) for i in range(ends)])  26.5 us
    ppermute x8, starting transfers between devices, padded_2(): lax.ppermute(tail, axis, [(i, (i + 1) % count) for i in range(ends)])  25.2 us
  transfers between devices with their start and end apart: 20, of which 12 were waited for; matrix products, arithmetic and copies ran while one was open for 1% of the time, Pallas kernels for 0%

profile of v1, /device:TPU:1, one launch (start us, length us, event | category | flops | bytes accessed | tf_op | source)
XLA Modules:
  0.0 1098.1 jit_solution(14748428521687084278)
XLA Ops:
  6.5 1.3 fusion.70
  11.7 1.4 constant_dynamic-slice_fusion.4
  14.4 2.4 convert_reduce_fusion
  17.7 13.4 %while.60 = (s32[]{:T(128)}, f32[512,128]{1,0:T(8,128)S(1)}, f32[512,128]{1,0:T(8,128)}, s32[]{:T(128)}, s32[512]{0:T(512)S(1)}, /*index=5*/s32[512]{0:T(512)S(1...) while((s32[]{:T(128)}, f32[512,128]{1,0:T(8,128)S(1)}, ...), condition=%wide.region_4.5_spmd.clone, body=%wide.region_1.4_spmd.clone.sunk | while | flops 4265478 | bytes 13388487 | solution.py:97
  17.8 3.0 gather_fusion
  21.6 4.4 fusion.99
  26.6 1.4 scatter_custom_fusion.42
  28.0 3.1 scatter_custom_fusion.43
  31.1 1.6 convert_element_type.93
  36.0 118.7 %all-gather.5.cloned.1.call-done = bf16[16384,128]{1,0:T(8,128)(2,1)} async-done(((bf16[512,128]{1,0:T(8,128)(2,1)}), bf16[16384,128]{1,0:T(8,128)(2,1)}) %all-gather.5.cloned.1.call-update) | async-done | bytes 4194320 | tf_op jit(solution)/shard_map/all_gather | solution.py:14
  154.7 2.8 reduce_sum.88
  157.5 137.6 %all-reduce.8.cloned.1.call-done = bf16[512,128]{1,0:T(8,128)(2,1)} async-done(((bf16[512,128]{1,0:T(8,128)(2,1)}), bf16[512,128]{1,0:T(8,128)(2,1)}) %all-reduce.8.cloned.1.call-update) | async-done | bytes 131088 | tf_op jit(solution)/shard_map/psum | solution.py:102
  297.8 14.1 %while.61 = (s32[]{:T(128)}, f32[1024,128]{1,0:T(8,128)}, f32[1024,128]{1,0:T(8,128)}, s32[]{:T(128)}, s32[512]{0:T(512)S(1)}, /*index=5*/s32[512]{0:T(512)S(1)}...) while((s32[]{:T(128)}, f32[1024,128]{1,0:T(8,128)}, ...), condition=%wide.region_11.12_spmd.clone, body=%wide.region_8.11_spmd.clone.sunk | while | flops 4265478 | bytes 13912775 | solution.py:122
  297.9 3.0 gather_fusion.2
  301.6 3.4 fusion.104
  305.6 3.1 scatter_custom_fusion.46
  308.7 3.2 scatter_custom_fusion.47
  311.9 2.1 add_divide_fusion.1
  314.0 2.0 reshape.54
  316.0 2.0 fusion.65
  320.4 14.9 %while.62 = (s32[]{:T(128)}, f32[512,128]{1,0:T(8,128)}, f32[512,128]{1,0:T(8,128)}, s32[]{:T(128)}, s32[512]{0:T(512)S(1)}, /*index=5*/s32[512]{0:T(512)S(1)}, ...) while((s32[]{:T(128)}, f32[512,128]{1,0:T(8,128)}, ...), condition=%wide.region_15.16_spmd.clone, body=%wide.region_12.15_spmd.clone.sunk | while | flops 4265478 | bytes 13388487 | solution.py:97
  320.5 3.0 gather_fusion.4
  324.3 4.4 fusion.109
  329.4 2.9 scatter_custom_fusion.50
  332.3 3.1 scatter_custom_fusion.51
  335.3 1.6 convert_element_type.99
  337.2 1.6 convert_element_type.97
  339.6 164.2 %all-gather.7.cloned.1.call-done = bf16[16384,128]{1,0:T(8,128)(2,1)} async-done(((bf16[512,128]{1,0:T(8,128)(2,1)}), bf16[16384,128]{1,0:T(8,128)(2,1)}) %all-gather.7.cloned.1.call-update) | async-done | bytes 4194320 | tf_op jit(solution)/shard_map/all_gather | solution.py:14
  503.9 2.8 reduce_sum.90
  506.7 137.8 %all-reduce.10.cloned.1.call-done = bf16[512,128]{1,0:T(8,128)(2,1)} async-done(((bf16[512,128]{1,0:T(8,128)(2,1)}), bf16[512,128]{1,0:T(8,128)(2,1)}) %all-reduce.10.cloned.1.call-update) | async-done | bytes 131088 | tf_op jit(solution)/shard_map/psum | solution.py:102
  646.3 12.7 %while.63 = (s32[]{:T(128)}, f32[1024,128]{1,0:T(8,128)S(1)}, f32[1024,128]{1,0:T(8,128)}, s32[]{:T(128)}, s32[512]{0:T(512)S(1)}, /*index=5*/s32[512]{0:T(512)S...) while((s32[]{:T(128)}, f32[1024,128]{1,0:T(8,128)S(1)}, ...), condition=%wide.region_21.22_spmd.clone, body=%wide.region_18.21_spmd.clone.sunk | while | flops 4265478 | bytes 13912775 | solution.py:122
  646.4 3.0 gather_fusion.6
  650.1 3.4 fusion.114
  654.2 1.5 scatter_custom_fusion.54
  655.7 3.3 scatter_custom_fusion.55
  661.2 7.4 collective-permute-start
  668.6 1.9 collective-permute-start.1
  670.5 3.1 collective-permute-done.1
  673.7 3.1 collective-permute-start.2
  676.8 1.3 collective-permute-start.3
  678.1 3.4 collective-permute-done.3
  683.3 1.5 multiply_reduce_fusion.3
  684.8 112.3 %all-reduce.4 = (f32[]{:T(128)}, f32[]{:T(128)}) all-reduce(f32[]{:T(128)} %get-tuple-element.835, f32[]{:T(128)} %get-tuple-element.833), channel_id=1, replica_groups=mesh['gz'=8,'gx'=32] {'gz','gx'}, use_global_device_ids=true, to_apply=%region_23.24 | all-reduce | flops 2 | bytes 16 | tf_op jit(solution)/shard_map/psum | solution.py:128
  798.6 3.5 collective-permute-start.4
  802.1 1.9 collective-permute-start.5
  804.0 3.1 collective-permute-done.5
  807.2 1.4 collective-permute-start.6
  809.9 3.6 collective-permute-done.7
  815.3 1.4 multiply_reduce_fusion.2
  816.8 77.7 %psum.53 = f32[]{:T(128)} all-reduce(f32[]{:T(128)} %get-tuple-element.829), channel_id=1, replica_groups=mesh['gz'=8,'gx'=32] {'gz','gx'}, use_global_device_ids=true, to_apply=%region_27.28 | all-reduce | flops 1 | bytes 8 | tf_op jit(solution)/shard_map/psum | solution.py:137
  895.3 3.5 collective-permute-start.8
  898.7 2.1 collective-permute-start.9
  900.9 2.9 collective-permute-done.9
  903.8 1.4 collective-permute-start.10
  906.6 3.6 collective-permute-done.11
  912.0 1.4 multiply_reduce_fusion.1
  913.4 78.8 %psum.54 = f32[]{:T(128)} all-reduce(f32[]{:T(128)} %get-tuple-element.825), channel_id=1, replica_groups=mesh['gz'=8,'gx'=32] {'gz','gx'}, use_global_device_ids=true, to_apply=%region_29.30 | all-reduce | flops 1 | bytes 8 | tf_op jit(solution)/shard_map/psum | solution.py:137
  993.0 3.5 collective-permute-start.12
  996.5 1.9 collective-permute-start.13
  998.4 3.1 collective-permute-done.13
  1001.6 1.4 collective-permute-start.14
  1004.3 3.6 collective-permute-done.15
  1009.7 1.4 multiply_reduce_fusion
  1011.2 78.8 %psum.55 = f32[]{:T(128)} all-reduce(f32[]{:T(128)} %get-tuple-element.821), channel_id=1, replica_groups=mesh['gz'=8,'gx'=32] {'gz','gx'}, use_global_device_ids=true, to_apply=%region_31.32 | all-reduce | flops 1 | bytes 8 | tf_op jit(solution)/shard_map/psum | solution.py:137
  (97 shorter events, 32.5 us)
Async XLA Ops:
  6.5 10.2 copy-start.1
  6.5 148.2 %all-gather.5.cloned.1.call-start = ((), (), s32[]{:S(2)}) async-start(), calls=%async_computation.2 | async-start | bytes 4325376 | tf_op jit(solution)/shard_map/all_gather | solution.py:14
  14.4 2.6 copy-start.4
  14.4 2.6 copy-start.5
  14.4 3.4 copy-start
  32.7 262.4 %all-reduce.8.cloned.1.call-start = ((), (), s32[]{:S(2)}) async-start(), calls=%async_computation | async-start | bytes 262144 | tf_op jit(solution)/shard_map/psum | solution.py:102
  33.5 470.4 %all-gather.7.cloned.1.call-start = ((), (), s32[]{:S(2)}) async-start(), calls=%async_computation.3 | async-start | bytes 4325376 | tf_op jit(solution)/shard_map/all_gather | solution.py:14
  337.0 307.5 %all-reduce.10.cloned.1.call-start = ((), (), s32[]{:S(2)}) async-start(), calls=%async_computation.1 | async-start | bytes 262144 | tf_op jit(solution)/shard_map/psum | solution.py:102
  503.9 140.6 %copy-start.3 = (f32[512,128]{1,0:T(8,128)S(1)}, f32[512,128]{1,0:T(8,128)}, u32[]{:S(2)}) copy-start(f32[512,128]{1,0:T(8,128)} %reshape.55) | copy-start | bytes 786436
  659.0 1.3 copy-start.2
  661.2 9.3 collective-permute-start
  668.6 5.1 collective-permute-start.1
  673.7 4.4 collective-permute-start.2
  676.8 4.7 collective-permute-start.3
  798.6 5.5 collective-permute-start.4
  802.1 5.1 collective-permute-start.5
  807.2 2.7 collective-permute-start.6
  808.6 4.9 collective-permute-start.7
  895.3 5.6 collective-permute-start.8
  898.7 5.1 collective-permute-start.9
  903.8 2.7 collective-permute-start.10
  905.2 4.9 collective-permute-start.11
  993.0 5.4 collective-permute-start.12
  996.5 5.1 collective-permute-start.13
  1001.6 2.7 collective-permute-start.14
  1003.0 4.9 collective-permute-start.15
Sparse Core Ops, SparseCore 0:
  32.9 121.8 all-gather.4
  158.2 136.8 all-reduce.7
  337.1 166.6 all-gather.6
  507.6 136.8 all-reduce.9
